TPU v7x, 128 devices: a whole 4x4x4 slice. The times are simulated.
128 devices in a mesh: row: 4 (over x), col: 16 (over z, y), depth: 2 (over core).
Axes of the slice: x: 4, y: 4, z: 4, core: 2. Of those that a mesh axis runs over, the one named last changes fastest.
Arguments:
- tokens: bfloat16 [2048, 8192], P('depth', 'col'), may hold values from -6 to 6
- weight: bfloat16 [8192, 14336], P('col', ('row', 'depth')), may hold values from -0.0625 to 0.0625
- block_mask: int32 [64, 112], replicated, may hold values 0 or 1
- cotangent: bfloat16 [2048, 14336], P('depth', 'row'), may hold values from -6 to 6
- example_ids: int32 [2048], replicated, may hold values from 0 to 3, as said below
Outputs:
- outputs: bfloat16 [2048, 14336], P('depth', 'row')
- grad_in: bfloat16 [2048, 8192], P('depth', 'col')
- grad_weight: bfloat16 [8192, 14336], P('col', ('row', 'depth'))
Inputs may be any that keep to these rules, and one draw needn't show every extreme that they name: `example_ids`: in the b-th aligned block of 1024 tokens (b from 0), the ids are 2 b for a first run of tokens and 2 b + 1 for the rest; each example has at least 128 tokens, and in every draw some example has exactly 896.
All inputs are finite; a program needn't handle non-finite values.
Results may differ from a plain program's by a relative error of at most 0.0052.
Values may be sent and summed in bfloat16 or wider, within the bound.
A program may use at most 128 MiB of HBM per device.

v0:
```python
import math
import jax
import jax.numpy as jnp
from jax import lax
from jax.sharding import PartitionSpec as P

D = 8192
FW = 14336
BLOCK = 128
TOK_DEV = 1024
EX_DEV = 2


def total_squares(partial_squares):
    return lax.psum(partial_squares, ("row", "col"))


def shards(tokens, weight, block_mask, cotangent, example_ids):
    tok_rows = tokens.shape[0]
    width_here = tokens.shape[1]
    hidden_here = cotangent.shape[1]
    col_at = lax.axis_index("col")
    row_at = lax.axis_index("row")
    depth_at = lax.axis_index("depth")
    tile_mask = lax.dynamic_slice(
        block_mask,
        (col_at * (width_here // BLOCK), row_at * (hidden_here // BLOCK)),
        (width_here // BLOCK, hidden_here // BLOCK),
    )
    keep = jnp.repeat(jnp.repeat(tile_mask > 0, BLOCK, axis=0), BLOCK, axis=1)
    zero_half = jnp.zeros((), jnp.bfloat16)
    ids_here = lax.dynamic_slice_in_dim(example_ids, depth_at * tok_rows, tok_rows)
    per_grads = []
    squares = []
    for slot in range(EX_DEV):
        chosen = ids_here == depth_at * EX_DEV + slot
        picked = jnp.where(chosen[:, None], cotangent, zero_half)
        product = lax.dot_general(
            tokens, picked, (((0,), (0,)), ((), ())), preferred_element_type=jnp.float32
        )
        product = jnp.where(keep, product, jnp.float32(0.0))
        per_grads.append(product)
        squares.append(jnp.sum(product * product))
    partial_squares = jnp.stack(squares)
    kept = keep
    out_part = jnp.dot(
        tokens,
        jnp.where(kept, lax.all_gather(weight, "depth", axis=1, tiled=True), zero_half),
        preferred_element_type=jnp.float32,
    )
    kept = keep
    masked_piece = jnp.where(kept, lax.all_gather(weight, "depth", axis=1, tiled=True), zero_half)
    back_part = lax.dot_general(
        cotangent, masked_piece, (((1,), (1,)), ((), ())), preferred_element_type=jnp.float32
    )
    out_sum = lax.psum(out_part, "col")
    back_sum = lax.psum(back_part, "row")
    all_squares = total_squares(partial_squares)
    out_final = out_sum.astype(jnp.bfloat16)
    back_final = back_sum.astype(jnp.bfloat16)
    bound = jnp.float32(0.5 * math.sqrt(D * FW * TOK_DEV))
    norms = jnp.sqrt(all_squares)
    factors = bound / jnp.maximum(norms, bound)
    examples_all = EX_DEV * lax.axis_size("depth")
    combined = jnp.zeros((width_here, hidden_here), jnp.float32)
    for slot in range(EX_DEV):
        combined = combined + factors[slot] * per_grads[slot]
    combined = combined / examples_all
    grad_sum = lax.psum_scatter(
        combined.astype(jnp.bfloat16), "depth", scatter_dimension=1, tiled=True
    )
    return (out_final, back_final, grad_sum)


def solution(mesh):
    placed = (P("depth", "col"), P("col", ("row", "depth")), P(), P("depth", "row"), P())
    return jax.shard_map(
        shards,
        mesh=mesh,
        in_specs=placed,
        out_specs=(P("depth", "row"), P("depth", "col"), P("col", ("row", "depth"))),
        check_vma=False,
    )
```

profile of v0, /device:TPU:0, one launch (start us, length us, event | category | flops | bytes accessed | tf_op | source)
XLA Modules:
  0.0 582.8 jit_solution(15162042323849801208)
XLA Ops:
  7.2 0.0 copy-start
  7.2 0.0 all-gather.2.cloned.1.call-start
  7.2 3.9 copy.9
  11.1 0.0 all-gather.2.cloned.1.call-update
  11.2 0.0 reduce-scatter.2.cloned.1.call-start
  11.2 0.8 dynamic-slice_compare_fusion.2
  12.0 0.1 copy.8
  12.1 0.1 broadcast_bitcast_fusion
  12.3 0.7 dynamic-slice_compare_fusion
  13.0 0.0 copy-done
  13.0 6.5 %fusion = f32[3584,512]{1,0:T(8,128)S(1)} fusion(bf16[1024,512]{1,0:T(8,128)(2,1)S(1)} %copy-done, bf16[1024,3584]{1,0:T(8,128)(2,1)} %param.8, pred[1024]{0:T(1024)(128)(4,1)S(1)} %get-tuple-element.8), kind=kOutput, calls=%fused_computation.6 | convolution fusion | flops 3761766400 | bytes 15729664 | tf_op jit(solution)/shard_map/dot_general | solution.py:38
  19.5 0.0 copy-start.1
  19.5 14.7 %multiply_reduce_fusion.1 = (f32[]{:T(128)}, f32[]{:T(128)}, f32[3584,512]{1,0:T(8,128)}) fusion(pred[512,28]{0,1:T(8,128)(4,1)S(1)} %bitcast.44, f32[3584,512]{1,0:T(8,128)S(1)} %fusion, bf16[1024,512]{1,0:T(8,128)(2,1)S(1)} %copy-done, bf16[1024,3584]{1,0:T(8,128)(2,1)} %param.8, pred[1024]{0:T(1024)(128)(4,1)S(1)} %get-tuple-element.9), kind=kOutput, calls=%fused_computation.8 | convolution fusion | flops 3772776448 | bytes 23084040 | tf_op jit(solution)/shard_map/dot_general | solution.py:38
  34.2 0.0 copy-done.1
  34.2 1.3 pad_maximum_fusion
  35.5 180.6 %psum.23 = f32[2]{0:T(128)S(1)} all-reduce(f32[2]{0:T(128)S(1)} %pad_maximum_fusion), channel_id=1, replica_groups=mesh['row'=4,'col'=16,'depth'=2] {'row','col'}, use_global_device_ids=true, to_apply=%region_4.5 | all-reduce | flops 2 | bytes 16 | tf_op jit(solution)/shard_map/psum | solution.py:15
  216.1 0.6 fusion.10
  216.7 9.2 %multiply_convert_fusion = bf16[512,3584]{0,1:T(8,128)(2,1)} fusion(f32[3584,512]{1,0:T(8,128)} %get-tuple-element.12, f32[3584,512]{1,0:T(8,128)} %copy-done.1, f32[]{:T(128)} %bitcast.8, f32[]{:T(128)} %bitcast.7, pred[512,28]{0,1:T(8,128)(4,1)S(1)} %bitcast.45), kind=kLoop, calls=%fused_computation.4 | loop fusion | flops 12845056 | bytes 18364424 | tf_op jit(solution)/shard_map/convert_element_type | solution.py:70
  225.9 0.0 reduce-scatter.2.cloned.1.call-update
  225.9 0.0 all-gather.2.cloned.1.call-done
  226.0 2.3 bitcast_select_fusion.2
  228.3 7.8 %convolution_bitcast_fusion.1 = f32[1024,512]{0,1:T(8,128)} fusion(bf16[512,3584]{0,1:T(8,128)(2,1)S(1)} %bitcast_select_fusion.2, bf16[1024,3584]{1,0:T(8,128)(2,1)} %param.8), kind=kOutput, calls=%fused_computation.15 | convolution fusion | flops 3758096384 | bytes 13107200 | tf_op jit(solution)/shard_map/dot_general | solution.py:53
  236.1 7.3 %convolution_bitcast_fusion = f32[1024,3584]{0,1:T(8,128)} fusion(bf16[512,3584]{0,1:T(8,128)(2,1)S(1)} %bitcast_select_fusion.2, bf16[1024,512]{1,0:T(8,128)(2,1)S(1)} %copy-done), kind=kOutput, calls=%fused_computation.3 | convolution fusion | flops 3758096384 | bytes 19398656 | tf_op jit(solution)/shard_map/dot_general | solution.py:46
  243.4 31.6 %all-reduce.2 = bf16[1024,512]{0,1:T(8,128)(2,1)S(1)} all-reduce(f32[1024,512]{0,1:T(8,128)} %convolution_bitcast_fusion.1), channel_id=1, replica_groups=mesh['row'=4,'col'=16,'depth'=2] {'row'}, use_global_device_ids=true, to_apply=%region_1.2 | all-reduce | flops 524288 | bytes 3145728 | tf_op jit(solution)/shard_map/psum | solution.py:57
  275.0 1.3 copy.11
  276.4 285.8 %all-reduce.3 = bf16[1024,3584]{0,1:T(8,128)(2,1)} all-reduce(f32[1024,3584]{0,1:T(8,128)} %convolution_bitcast_fusion), channel_id=1, replica_groups=mesh['row'=4,'col'=16,'depth'=2] {'col'}, use_global_device_ids=true, to_apply=%region_0.1 | all-reduce | flops 3670016 | bytes 22020096 | tf_op jit(solution)/shard_map/psum | solution.py:56
  562.2 9.9 %copy.10 = bf16[1024,3584]{1,0:T(8,128)(2,1)} copy(bf16[1024,3584]{0,1:T(8,128)(2,1)} %all-reduce.3) | data formatting | bytes 14680064
  572.1 0.0 reduce-scatter.2.cloned.1.call-done
  572.1 3.8 copy.12
  (3 shorter events, 0.0 us)
Async XLA Ops:
  7.2 5.8 copy-start
  7.2 218.8 %all-gather.2.cloned.1.call-start = ((), (), s32[]{:S(2)}) async-start(), calls=%async_computation.1 | async-start | bytes 5505024 | tf_op jit(solution)/shard_map/all_gather | solution.py:48
  11.2 561.0 %reduce-scatter.2.cloned.1.call-start = ((), (), s32[]{:S(2)}) async-start(), calls=%async_computation.2 | async-start | bytes 5505024 | tf_op jit(solution)/shard_map/reduce_scatter | solution.py:69
  19.5 14.8 %copy-start.1 = (f32[3584,512]{1,0:T(8,128)}, f32[3584,512]{1,0:T(8,128)S(1)}, u32[]{:S(2)}) copy-start(f32[3584,512]{1,0:T(8,128)S(1)} %fusion) | copy-start | bytes 22020100
Sparse Core Ops, SparseCore 0:
  11.3 18.0 all-gather.1
  226.0 8.0 reduce-scatter.1
where the time goes:
time: 583 us
  blocking collectives  498 us (85%)
  matrix products  36.3 us (6%)
  local copies, waits for them, and re-layouts  19.8 us (3%)
  other arithmetic  14.3 us (2%)
  between operations  14.1 us (2%)
    psum x1, blocking collectives, shards(): out_sum = lax.psum(out_part, 'col')  286 us
    psum x1, blocking collectives, total_squares(): return lax.psum(partial_squares, ('row', 'col'))  181 us
    psum x1, blocking collectives, shards(): back_sum = lax.psum(back_part, 'row')  31.6 us
    dot_general x2, matrix products, shards(): lax.dot_general(tokens, picked, (((0,), (0,)), ((), ())), preferred_eleme...  21.2 us
    unnamed x11, local copies, waits for them, and re-layouts  19.1 us
  transfers between devices with their start and end apart: 2, of which 0 were waited for; matrix products, arithmetic and copies ran while one was open for 11% of the time, Pallas kernels for 0%

commit v1 on v0

--- a/solution.py
+++ b/solution.py
@@ -1,3 +1,4 @@
+import functools
 import math
 import jax
 import jax.numpy as jnp
@@ -9,6 +10,18 @@
 BLOCK = 128
 TOK_DEV = 1024
 EX_DEV = 2
+
+
+def read_squares(patch, ax_name):
+    clean = patch
+    num = lax.axis_size(ax_name)
+    for dev_i in [[(d, d ^ k) for d in range(num)] for k in (1, 2, 4, 8, 16) if k < num]:
+        mid_arr = lax.ppermute(clean, axis_name=ax_name, perm=dev_i)
+        clean = clean + mid_arr
+    return clean
+
+
+turn_turns = functools.partial(read_squares, ax_name="col")
 
 
 def total_squares(partial_squares):
@@ -53,7 +66,7 @@
     back_part = lax.dot_general(
         cotangent, masked_piece, (((1,), (1,)), ((), ())), preferred_element_type=jnp.float32
     )
-    out_sum = lax.psum(out_part, "col")
+    out_sum = turn_turns(out_part)
     back_sum = lax.psum(back_part, "row")
     all_squares = total_squares(partial_squares)
     out_final = out_sum.astype(jnp.bfloat16)

time: 583 us -> 1360 us (2.33)
  waiting for transfers between devices: 0.06 us -> 1020 us
  blocking collectives: 498 us -> 211 us
  other arithmetic: 14.3 us -> 48.5 us
    ppermute x0 -> x4, waiting for transfers between devices: none -> 1000 us  [read_squares(): mid_arr = lax.ppermute(clean, axis_name=ax_name, perm=dev_i)]
    psum x1 -> x0, blocking collectives: 286 us -> none  [shards(): out_sum = lax.psum(out_part, 'col')]
    add x0 -> x3, other arithmetic: none -> 21.4 us  [read_squares(): clean = clean + mid_arr]
    all_gather x1, waiting for transfers between devices: 0.02 us -> 17.1 us  [shards(): lax.all_gather(weight, 'depth', axis=1, tiled=True)]
  transfers between devices with their start and end apart: 2 -> 6, of which waited for: 0 -> 5; matrix products, arithmetic and copies ran while one was open for 11% -> 4% of each run, Pallas kernels for 0% -> 0%
where the time goes in v1:
time: 1360 us
  waiting for transfers between devices  1020 us (75%)
  blocking collectives  211 us (16%)
  other arithmetic  48.5 us (4%)
  matrix products  35.7 us (3%)
  local copies, waits for them, and re-layouts  19.8 us (1%)
  between operations  14.2 us (1%)
    ppermute x4, waiting for transfers between devices, read_squares(): mid_arr = lax.ppermute(clean, axis_name=ax_name, perm=dev_i)  1000 us
    psum x1, blocking collectives, total_squares(): return lax.psum(partial_squares, ('row', 'col'))  179 us
    psum x1, blocking collectives, shards(): back_sum = lax.psum(back_part, 'row')  31.6 us
  transfers between devices with their start and end apart: 6, of which 5 were waited for; matrix products, arithmetic and copies ran while one was open for 4% of the time, Pallas kernels for 0%

profile of v1, /device:TPU:0, one launch (start us, length us, event | category | flops | bytes accessed | tf_op | source)
XLA Modules:
  0.0 1359.7 jit_solution(6343700674889137479)
XLA Ops:
  7.2 0.0 copy-start
  7.2 0.0 all-gather.2.cloned.1.call-start
  7.2 3.9 copy.9
  11.1 0.0 all-gather.2.cloned.1.call-update
  11.2 0.0 reduce-scatter.2.cloned.1.call-start
  11.2 0.8 dynamic-slice_compare_fusion.2
  12.0 0.1 copy.8
  12.1 0.1 broadcast_bitcast_fusion
  12.3 17.1 %all-gather.2.cloned.1.call-done = bf16[512,3584]{0,1:T(8,128)(2,1)} async-done(((bf16[512,1792]{0,1:T(8,128)(2,1)}), bf16[512,3584]{0,1:T(8,128)(2,1)}) %all-gather.2.cloned.1.call-update) | async-done | bytes 3670032 | tf_op jit(solution)/shard_map/all_gather | solution.py:61
  29.4 2.3 bitcast_select_fusion.2
  31.7 0.0 copy-done
  31.7 0.0 copy-start.2
  31.7 4.3 convolution_bitcast_fusion
  36.0 0.0 copy-done.2
  36.1 1.7 collective-permute-start
  37.7 316.0 %collective-permute-done = f32[1024,3584]{0,1:T(8,128)} collective-permute-done((f32[1024,3584]{0,1:T(8,128)S(1)}, f32[1024,3584]{0,1:T(8,128)}, u32[]{:S(2)}, u32[]{:S(2)}) %collective-permute-start) | collective-permute-done | bytes 14680096 | tf_op jit(solution)/shard_map/ppermute | solution.py:19
  353.7 7.2 add.35
  360.9 3.2 collective-permute-start.1
  364.1 315.1 %collective-permute-done.1 = f32[1024,3584]{0,1:T(8,128)} collective-permute-done((f32[1024,3584]{0,1:T(8,128)S(1)}, f32[1024,3584]{0,1:T(8,128)}, u32[]{:S(2)}, u32[]{:S(2)}) %collective-permute-start.1) | collective-permute-done | bytes 14680096 | tf_op jit(solution)/shard_map/ppermute | solution.py:19
  679.2 7.2 add.36
  686.4 0.0 copy-start.3
  686.4 1.7 collective-permute-start.2
  688.1 314.1 %collective-permute-done.2 = f32[1024,3584]{0,1:T(8,128)S(1)} collective-permute-done((f32[1024,3584]{0,1:T(8,128)S(1)}, f32[1024,3584]{0,1:T(8,128)S(1)}, u32[]{:S(2)}, u32[]{:S(2)}) %collective-permute-start.2) | collective-permute-done | bytes 14680096 | tf_op jit(solution)/shard_map/ppermute | solution.py:19
  1002.2 7.0 add.37
  1009.3 3.2 collective-permute-start.3
  1012.5 0.0 copy-done.3
  1012.5 6.5 fusion
  1019.0 0.0 copy-start.1
  1019.0 14.2 %multiply_reduce_fusion.1 = (f32[]{:T(128)}, f32[]{:T(128)}, f32[3584,512]{1,0:T(8,128)}) fusion(pred[512,28]{0,1:T(8,128)(4,1)S(1)} %bitcast.45, f32[3584,512]{1,0:T(8,128)S(1)} %fusion, bf16[1024,512]{1,0:T(8,128)(2,1)S(1)} %copy-done, bf16[1024,3584]{1,0:T(8,128)(2,1)} %param.8, pred[1024]{0:T(1024)(128)(4,1)S(1)} %get-tuple-element.9), kind=kOutput, calls=%fused_computation.9 | convolution fusion | flops 3772776448 | bytes 23084040 | tf_op jit(solution)/shard_map/dot_general | solution.py:51
  1033.2 0.0 copy-done.1
  1033.2 1.4 pad_maximum_fusion
  1034.6 179.4 %psum.15 = f32[2]{0:T(128)S(1)} all-reduce(f32[2]{0:T(128)S(1)} %pad_maximum_fusion), channel_id=1, replica_groups=mesh['row'=4,'col'=16,'depth'=2] {'row','col'}, use_global_device_ids=true, to_apply=%region_3.4 | all-reduce | flops 2 | bytes 16 | tf_op jit(solution)/shard_map/psum | solution.py:28
  1213.9 0.6 fusion.10
  1214.5 9.3 multiply_convert_fusion
  1223.9 0.0 reduce-scatter.2.cloned.1.call-update
  1223.9 10.7 convolution_bitcast_fusion.1
  1234.6 31.6 %all-reduce.1 = bf16[1024,512]{0,1:T(8,128)(2,1)S(1)} all-reduce(f32[1024,512]{0,1:T(8,128)} %convolution_bitcast_fusion.1), channel_id=1, replica_groups=mesh['row'=4,'col'=16,'depth'=2] {'row'}, use_global_device_ids=true, to_apply=%region_0.1 | all-reduce | flops 524288 | bytes 3145728 | tf_op jit(solution)/shard_map/psum | solution.py:70
  1266.3 1.3 copy.11
  1267.6 0.0 reduce-scatter.2.cloned.1.call-done
  1267.6 3.8 copy.12
  1271.4 58.1 %collective-permute-done.3 = f32[1024,3584]{0,1:T(8,128)} collective-permute-done((f32[1024,3584]{0,1:T(8,128)}, f32[1024,3584]{0,1:T(8,128)}, u32[]{:S(2)}, u32[]{:S(2)}) %collective-permute-start.3) | collective-permute-done | bytes 14680096 | tf_op jit(solution)/shard_map/ppermute | solution.py:19
  1329.5 13.4 add_convert_fusion
  1342.9 9.9 copy.10
  (4 shorter events, 0.1 us)
Async XLA Ops:
  7.2 24.5 %copy-start = (bf16[1024,512]{1,0:T(8,128)(2,1)S(1)}, bf16[1024,512]{1,0:T(8,128)(2,1)}, u32[]{:S(2)}) copy-start(bf16[1024,512]{1,0:T(8,128)(2,1)} %param.5) | copy-start | bytes 3145732
  7.2 22.2 %all-gather.2.cloned.1.call-start = ((), (), s32[]{:S(2)}) async-start(), calls=%async_computation.1 | async-start | bytes 5505024 | tf_op jit(solution)/shard_map/all_gather | solution.py:61
  11.2 1256.4 %reduce-scatter.2.cloned.1.call-start = ((), (), s32[]{:S(2)}) async-start(), calls=%async_computation.2 | async-start | bytes 5505024 | tf_op jit(solution)/shard_map/reduce_scatter | solution.py:82
  31.7 4.3 copy-start.2
  36.1 317.7 %collective-permute-start = (f32[1024,3584]{0,1:T(8,128)S(1)}, f32[1024,3584]{0,1:T(8,128)}, u32[]{:S(2)}, u32[]{:S(2)}) collective-permute-start(f32[1024,3584]{0,1:T(8,128)S(1)} %convolution_bitcast_fusion), channel_id=1, source_target_pairs={{0,2},{2,0},{4,6},{6,4},{8,10},{10,8},{12,14},{14,12},{16,18},{18,... | collective-permute-start | bytes 44040200 | tf_op jit(solution)/shard_map/ppermute | solution.py:19
  360.9 318.3 %collective-permute-start.1 = (f32[1024,3584]{0,1:T(8,128)S(1)}, f32[1024,3584]{0,1:T(8,128)}, u32[]{:S(2)}, u32[]{:S(2)}) collective-permute-start(f32[1024,3584]{0,1:T(8,128)S(1)} %add.35), channel_id=1, source_target_pairs={{0,4},{2,6},{4,0},{6,2},{8,12},{10,14},{12,8},{14,10},{16,20},{18,... | collective-permute-start | bytes 44040200 | tf_op jit(solution)/shard_map/ppermute | solution.py:19
  686.4 326.1 %copy-start.3 = (s32[2048]{0:T(1024)S(1)}, s32[2048]{0:T(1024)}, u32[]{:S(2)}) copy-start(s32[2048]{0:T(1024)} %param.9) | copy-start | bytes 24580
  686.4 315.8 %collective-permute-start.2 = (f32[1024,3584]{0,1:T(8,128)S(1)}, f32[1024,3584]{0,1:T(8,128)S(1)}, u32[]{:S(2)}, u32[]{:S(2)}) collective-permute-start(f32[1024,3584]{0,1:T(8,128)S(1)} %add.36), channel_id=1, source_target_pairs={{0,8},{2,10},{4,12},{6,14},{8,0},{10,2},{12,4},{14,6},{16,24},{18,... | collective-permute-start | bytes 44040200 | tf_op jit(solution)/shard_map/ppermute | solution.py:19
  1009.3 320.3 %collective-permute-start.3 = (f32[1024,3584]{0,1:T(8,128)}, f32[1024,3584]{0,1:T(8,128)}, u32[]{:S(2)}, u32[]{:S(2)}) collective-permute-start(f32[1024,3584]{0,1:T(8,128)} %add.37), channel_id=1, source_target_pairs={{0,16},{2,18},{4,20},{6,22},{8,24},{10,26},{12,28},{14,30},{16,0},... | collective-permute-start | bytes 44040200 | tf_op jit(solution)/shard_map/ppermute | solution.py:19
  1019.0 14.2 %copy-start.1 = (f32[3584,512]{1,0:T(8,128)}, f32[3584,512]{1,0:T(8,128)S(1)}, u32[]{:S(2)}) copy-start(f32[3584,512]{1,0:T(8,128)S(1)} %fusion) | copy-start | bytes 22020100
Sparse Core Ops, SparseCore 0:
  11.3 18.0 all-gather.1
  1224.0 8.0 reduce-scatter.1
